TPU v7x, 32 devices: a whole 2x2x4 slice. The times are simulated.
32 devices in a mesh: blk: 8 (over y, x, core), grp: 4 (over z).
Axes of the slice: x: 2, y: 2, z: 4, core: 2. Of those that a mesh axis runs over, the one named last changes fastest.
Arguments:
- points: bfloat16 [16, 4096], P(None, ('blk', 'grp')), may hold values from -2 to 2, as said below
- right_side: float32 [64, 4096], P(None, ('blk', 'grp')), may hold values from -10 to 16
- nugget: float32 [4096], P(('blk', 'grp')), may hold values from 2 to 3
- scales: float32 [16], replicated, may hold values from 0.8 to 1.25
- pairs: int32 [8, 3], replicated, may hold values 0 or 1
Outputs:
- solution: float32 [64, 4096], P(None, ('blk', 'grp'))
- residual: float32 [64, 4096], P(None, ('blk', 'grp'))
Inputs may be any that keep to these rules, and one draw needn't show every extreme that they name: pairs[b, d - 1] is 1 when block b and block (b + d) mod 8 share a tile. In features 0 and 1 the points of block b lie on the circle of radius 8 / (2 pi) about the anchor, at arc lengths from b to b + 3 + 1 (measured round the circle from feature 1 = 0), one point in each of 512 equal slots of that arc; features 2 to 15 lie between 0 and 0.3.
All inputs are finite; a program needn't handle non-finite values.
Results may differ from a plain program's by a relative error of at most 0.0006.
Values may be sent and summed in bfloat16 or wider, within the bound.
No kernel may reach another device: no remote copies, remote signals or barrier semaphores. Data moves between devices by JAX's collectives and lax.ppermute only.
A program may use at most 64 MiB of HBM per device.

v0:
```python
import jax
import jax.numpy as jnp
from jax import lax
from jax.sharding import PartitionSpec as P

ITERS = 2


def passed_along(block, axis, distance):
    devices = range(lax.axis_size(axis))
    route = [((i - distance) % len(devices), i) for i in devices]
    return lax.ppermute(block, axis, route)


def kernel_tile(row_z, col_z):
    cross = jnp.dot(
        row_z.T, col_z, precision=lax.Precision.HIGHEST, preferred_element_type=jnp.float32
    )
    squared = (
        jnp.sum(row_z * row_z, axis=0)[:, None]
        + jnp.sum(col_z * col_z, axis=0)[None, :]
        - 2.0 * cross
    )
    distance = jnp.sqrt(jnp.maximum(squared, 0.0))
    spare = jnp.maximum(1.0 - distance, 0.0)
    return (spare**4 * (4.0 * distance + 1.0)).astype(jnp.bfloat16)


def tile_terms(row_z, column_block, scales):
    feat = row_z.shape[0]
    col_z = column_block[:feat].astype(jnp.float32) / scales[:, None]
    col_vec = column_block[feat:]
    total = col_z.shape[1]
    width = min(512, total)
    count = total // width
    nrhs = col_vec.shape[0]
    rows = row_z.shape[1]

    def step(carry, index):
        ahead, behind = carry
        start = index * width
        part_z = lax.dynamic_slice_in_dim(col_z, start, width, 1)
        part_v = lax.dynamic_slice_in_dim(col_vec, start, width, 1)
        tile = kernel_tile(row_z, part_z)
        ahead = ahead + lax.dot_general(
            part_v, tile, (((1,), (1,)), ((), ())), preferred_element_type=jnp.float32
        )
        return ((ahead, behind), None)

    start_carry = (jnp.zeros((nrhs, rows), jnp.float32), jnp.zeros((nrhs, total), jnp.float32))
    result, unused = lax.scan(step, start_carry, jnp.arange(count, dtype=jnp.int32))
    return result


def on_device(points, right_side, nugget, scales, pairs):
    nblk = lax.axis_size("blk")
    ngrp = lax.axis_size("grp")
    rows = points.shape[1]
    maxp = pairs.shape[1]
    nrhs = right_side.shape[0]
    total = rows * ngrp
    here = lax.axis_index("blk")
    amp = 1.0 / (total + 16)
    own_z = points.astype(jnp.float32) / scales[:, None]

    def squares(values):
        return lax.psum(jnp.sum(values * values, axis=1), ("blk", "grp"))

    solution = jnp.zeros(right_side.shape, jnp.float32)
    residual = right_side
    direction = right_side
    norm_now = squares(residual)
    for step in range(ITERS):
        rounded = direction.astype(jnp.bfloat16)
        stacked = jnp.concatenate([points, rounded], axis=0)
        own = lax.all_gather(stacked, "grp", axis=1, tiled=True)
        forward, unused = tile_terms(own_z, own, scales)
        for offset in range(1, maxp + 1):
            for sign in (1, -1):
                fetch_offset = sign * offset
                partner = passed_along(own, "blk", -fetch_offset)
                owner = here if sign == 1 else (here - offset) % nblk
                active = lax.dynamic_index_in_dim(pairs[:, offset - 1], owner, keepdims=False) == 1
                column_block = partner
                ahead, unused = lax.cond(
                    active,
                    lambda: tile_terms(own_z, column_block, scales),
                    lambda: (
                        jnp.zeros((nrhs, rows), jnp.float32),
                        jnp.zeros((nrhs, total), jnp.float32),
                    ),
                )
                forward = forward + ahead
        image = nugget[None, :] * direction + amp * forward
        alpha = norm_now / lax.psum(jnp.sum(direction * image, axis=1), ("blk", "grp"))
        solution = solution + alpha[:, None] * direction
        residual = residual - alpha[:, None] * image
        if step + 1 < ITERS:
            norm_next = squares(residual)
            direction = residual + (norm_next / norm_now)[:, None] * direction
            norm_now = norm_next
    return (solution, residual)


def solution(mesh):
    placed = (P(None, ("blk", "grp")), P(None, ("blk", "grp")), P(("blk", "grp")), P(), P())
    return jax.shard_map(
        on_device,
        mesh=mesh,
        in_specs=placed,
        out_specs=(P(None, ("blk", "grp")), P(None, ("blk", "grp"))),
        check_vma=False,
    )
```

profile of v0, /device:TPU:0, one launch (start us, length us, event | category | flops | bytes accessed | tf_op | source)
XLA Modules:
  0.0 181.6 jit_solution(10527828224152508425)
XLA Ops:
  0.6 0.8 convert_element_type.149
  1.4 0.0 copy-start.1
  1.4 13.8 %all_gather.6 = bf16[80,512]{1,0:T(8,128)(2,1)S(1)} all-gather(bf16[80,128]{1,0:T(8,128)(2,1)S(1)} %pad_maximum_fusion.1), channel_id=1, replica_groups=mesh['blk'=8,'grp'=4] {'grp'}, dimensions={1}, use_global_device_ids=true | all-gather | bytes 102400 | tf_op jit(solution)/shard_map/all_gather | solution.py:76
  15.2 0.0 collective-permute-start.5
  15.2 1.7 collective-permute-start.4
  16.9 1.5 collective-permute-start.3
  18.4 1.4 collective-permute-start.2
  19.9 0.3 collective-permute-start.1
  20.1 0.1 multiply_reduce_fusion.30
  20.2 0.1 multiply_reduce_fusion.28
  20.3 0.6 multiply_convert_fusion.13
  21.0 0.0 copy-start.4
  21.0 0.2 fusion.92
  21.1 0.0 collective-permute-done.5
  21.1 2.4 %collective-permute-start = (bf16[80,512]{1,0:T(8,128)(2,1)S(1)}, bf16[80,512]{1,0:T(8,128)(2,1)S(1)}, u32[]{:S(2)}, u32[]{:S(2)}) collective-permute-start(bf16[80,512]{1,0:T(8,128)(2,1)S(1)} %all_gather.6), channel_id=1, source_target_pairs={{4,0},{8,4},{12,8},{16,12},{20,16},{24,20},{28,24},{0,28},{5,1},{9... | collective-permute-start | bytes 245768 | tf_op jit(solution)/shard_map/ppermute | solution.py:12
  23.6 0.7 constant_dynamic-slice_fusion.1
  26.8 0.7 constant_dynamic-slice_fusion.5
  28.7 1.1 conditional.17
  28.8 0.1 multiply_reduce_fusion.10
  28.9 0.8 multiply_convert_fusion.5
  29.6 0.2 convolution_bitcast_fusion.5
  29.8 0.0 collective-permute-done.4
  29.8 1.1 conditional.16
  29.8 0.1 multiply_reduce_fusion.8
  29.9 0.8 multiply_convert_fusion.4
  30.7 0.2 convolution_bitcast_fusion.4
  30.9 0.0 collective-permute-done.2
  31.0 1.1 conditional.13
  31.0 0.1 multiply_reduce_fusion.2
  31.1 0.8 multiply_convert_fusion.1
  31.9 0.2 convolution_bitcast_fusion.1
  32.0 0.0 copy-start
  32.1 0.0 copy-start.3
  32.1 0.7 copy-done
  32.8 0.1 multiply_reduce_fusion.27
  32.9 41.9 %all-reduce = (f32[64]{0:T(128)S(1)}, f32[64]{0:T(128)S(1)}) all-reduce(f32[64]{0:T(128)S(1)} %get-tuple-element.357, f32[64]{0:T(128)S(1)} %get-tuple-element.356), channel_id=1, replica_groups=mesh['blk'=8,'grp'=4] {'blk','grp'}, use_global_device_ids=true, to_apply=%region_1.0 | all-reduce | flops 128 | bytes 1024 | tf_op jit(solution)/shard_map/psum | solution.py:67
  74.8 0.2 multiply_reduce_fusion.26
  75.0 40.3 %psum.30 = f32[64]{0:T(128)S(1)} all-reduce(f32[64]{0:T(128)S(1)} %multiply_reduce_fusion.26), channel_id=1, replica_groups=mesh['blk'=8,'grp'=4] {'blk','grp'}, use_global_device_ids=true, to_apply=%region_31.32 | all-reduce | flops 64 | bytes 512 | tf_op jit(solution)/shard_map/psum | solution.py:67
  115.3 0.1 fusion.98
  115.5 12.1 %all_gather.7 = bf16[80,512]{1,0:T(8,128)(2,1)S(1)} all-gather(bf16[80,128]{1,0:T(8,128)(2,1)S(1)} %pad_maximum_fusion), channel_id=1, replica_groups=mesh['blk'=8,'grp'=4] {'grp'}, dimensions={1}, use_global_device_ids=true | all-gather | bytes 102400 | tf_op jit(solution)/shard_map/all_gather | solution.py:76
  127.6 1.7 collective-permute-start.10
  129.3 2.2 %collective-permute-start.9 = (bf16[80,512]{1,0:T(8,128)(2,1)S(1)}, bf16[80,512]{1,0:T(8,128)(2,1)S(1)}, u32[]{:S(2)}, u32[]{:S(2)}) collective-permute-start(bf16[80,512]{1,0:T(8,128)(2,1)S(1)} %all_gather.7), channel_id=1, source_target_pairs={{24,0},{28,4},{0,8},{4,12},{8,16},{12,20},{16,24},{20,28},{25,1},{... | collective-permute-start | bytes 245768 | tf_op jit(solution)/shard_map/ppermute | solution.py:12
  131.5 0.7 collective-permute-start.8
  132.2 0.0 collective-permute-start.7
  132.3 0.1 multiply_reduce_fusion.25
  132.4 0.6 multiply_convert_fusion.12
  133.0 2.7 %collective-permute-start.6 = (bf16[80,512]{1,0:T(8,128)(2,1)S(1)}, bf16[80,512]{1,0:T(8,128)(2,1)S(1)}, u32[]{:S(2)}, u32[]{:S(2)}) collective-permute-start(bf16[80,512]{1,0:T(8,128)(2,1)S(1)} %all_gather.7), channel_id=1, source_target_pairs={{4,0},{8,4},{12,8},{16,12},{20,16},{24,20},{28,24},{0,28},{5,1},{9... | collective-permute-start | bytes 245768 | tf_op jit(solution)/shard_map/ppermute | solution.py:12
  135.7 0.2 fusion.90
  135.9 1.1 conditional.23
  135.9 0.1 multiply_reduce_fusion.22
  136.0 0.8 multiply_convert_fusion.11
  136.8 0.2 convolution_bitcast_fusion.11
  136.9 1.1 conditional.22
  136.9 0.1 multiply_reduce_fusion.20
  137.0 0.8 multiply_convert_fusion.10
  137.8 0.2 convolution_bitcast_fusion.10
  138.1 0.3 collective-permute-done.7
  138.3 1.0 conditional.19
  138.3 0.1 multiply_reduce_fusion.14
  138.4 0.8 multiply_convert_fusion.7
  139.2 0.2 convolution_bitcast_fusion.7
  139.4 0.1 multiply_reduce_fusion.24
  139.5 41.3 %psum.31 = f32[64]{0:T(128)S(1)} all-reduce(f32[64]{0:T(128)S(1)} %get-tuple-element.360), channel_id=1, replica_groups=mesh['blk'=8,'grp'=4] {'blk','grp'}, use_global_device_ids=true, to_apply=%region_58.59 | all-reduce | flops 64 | bytes 512 | tf_op jit(solution)/shard_map/psum | solution.py:95
  180.8 0.7 multiply_subtract_fusion
  (38 shorter events, 0.4 us)
Async XLA Ops:
  0.6 0.8 copy-start.2
  1.4 18.7 %copy-start.1 = (f32[16]{0:T(128)S(1)}, f32[16]{0:T(128)}, u32[]{:S(2)}) copy-start(f32[16]{0:T(128)} %param.32) | copy-start | bytes 196
  15.2 5.9 %collective-permute-start.5 = (bf16[80,512]{1,0:T(8,128)(2,1)S(1)}, bf16[80,512]{1,0:T(8,128)(2,1)S(1)}, u32[]{:S(2)}, u32[]{:S(2)}) collective-permute-start(bf16[80,512]{1,0:T(8,128)(2,1)S(1)} %all_gather.6), channel_id=1, source_target_pairs={{20,0},{24,4},{28,8},{0,12},{4,16},{8,20},{12,24},{16,28},{21,1},{... | collective-permute-start | bytes 245768 | tf_op jit(solution)/shard_map/ppermute | solution.py:12
  15.2 14.6 %collective-permute-start.4 = (bf16[80,512]{1,0:T(8,128)(2,1)S(1)}, bf16[80,512]{1,0:T(8,128)(2,1)S(1)}, u32[]{:S(2)}, u32[]{:S(2)}) collective-permute-start(bf16[80,512]{1,0:T(8,128)(2,1)S(1)} %all_gather.6), channel_id=1, source_target_pairs={{12,0},{16,4},{20,8},{24,12},{28,16},{0,20},{4,24},{8,28},{13,1},{... | collective-permute-start | bytes 245768 | tf_op jit(solution)/shard_map/ppermute | solution.py:12
  16.9 13.9 %collective-permute-start.3 = (bf16[80,512]{1,0:T(8,128)(2,1)S(1)}, bf16[80,512]{1,0:T(8,128)(2,1)S(1)}, u32[]{:S(2)}, u32[]{:S(2)}) collective-permute-start(bf16[80,512]{1,0:T(8,128)(2,1)S(1)} %all_gather.6), channel_id=1, source_target_pairs={{24,0},{28,4},{0,8},{4,12},{8,16},{12,20},{16,24},{20,28},{25,1},{... | collective-permute-start | bytes 245768 | tf_op jit(solution)/shard_map/ppermute | solution.py:12
  18.4 12.5 %collective-permute-start.2 = (bf16[80,512]{1,0:T(8,128)(2,1)S(1)}, bf16[80,512]{1,0:T(8,128)(2,1)S(1)}, u32[]{:S(2)}, u32[]{:S(2)}) collective-permute-start(bf16[80,512]{1,0:T(8,128)(2,1)S(1)} %all_gather.6), channel_id=1, source_target_pairs={{8,0},{12,4},{16,8},{20,12},{24,16},{28,20},{0,24},{4,28},{9,1},{1... | collective-permute-start | bytes 245768 | tf_op jit(solution)/shard_map/ppermute | solution.py:12
  19.9 11.1 %collective-permute-start.1 = (bf16[80,512]{1,0:T(8,128)(2,1)S(1)}, bf16[80,512]{1,0:T(8,128)(2,1)S(1)}, u32[]{:S(2)}, u32[]{:S(2)}) collective-permute-start(bf16[80,512]{1,0:T(8,128)(2,1)S(1)} %all_gather.6), channel_id=1, source_target_pairs={{28,0},{0,4},{4,8},{8,12},{12,16},{16,20},{20,24},{24,28},{29,1},{... | collective-permute-start | bytes 245768 | tf_op jit(solution)/shard_map/ppermute | solution.py:12
  21.0 2.6 %copy-start.4 = (s32[8,3]{0,1:T(4,128)S(1)}, s32[8,3]{0,1:T(4,128)}, u32[]{:S(2)}) copy-start(s32[8,3]{0,1:T(4,128)} %param.33) | copy-start | bytes 292
  21.1 10.9 %collective-permute-start = (bf16[80,512]{1,0:T(8,128)(2,1)S(1)}, bf16[80,512]{1,0:T(8,128)(2,1)S(1)}, u32[]{:S(2)}, u32[]{:S(2)}) collective-permute-start(bf16[80,512]{1,0:T(8,128)(2,1)S(1)} %all_gather.6), channel_id=1, source_target_pairs={{4,0},{8,4},{12,8},{16,12},{20,16},{24,20},{28,24},{0,28},{5,1},{9... | collective-permute-start | bytes 245768 | tf_op jit(solution)/shard_map/ppermute | solution.py:12
  32.0 0.8 copy-start
  32.1 0.7 copy-start.3
  127.6 5.4 %collective-permute-start.11 = (bf16[80,512]{1,0:T(8,128)(2,1)S(1)}, bf16[80,512]{1,0:T(8,128)(2,1)S(1)}, u32[]{:S(2)}, u32[]{:S(2)}) collective-permute-start(bf16[80,512]{1,0:T(8,128)(2,1)S(1)} %all_gather.7), channel_id=1, source_target_pairs={{20,0},{24,4},{28,8},{0,12},{4,16},{8,20},{12,24},{16,28},{21,1},{... | collective-permute-start | bytes 245768 | tf_op jit(solution)/shard_map/ppermute | solution.py:12
  127.6 9.3 %collective-permute-start.10 = (bf16[80,512]{1,0:T(8,128)(2,1)S(1)}, bf16[80,512]{1,0:T(8,128)(2,1)S(1)}, u32[]{:S(2)}, u32[]{:S(2)}) collective-permute-start(bf16[80,512]{1,0:T(8,128)(2,1)S(1)} %all_gather.7), channel_id=1, source_target_pairs={{12,0},{16,4},{20,8},{24,12},{28,16},{0,20},{4,24},{8,28},{13,1},{... | collective-permute-start | bytes 245768 | tf_op jit(solution)/shard_map/ppermute | solution.py:12
  129.3 8.6 %collective-permute-start.9 = (bf16[80,512]{1,0:T(8,128)(2,1)S(1)}, bf16[80,512]{1,0:T(8,128)(2,1)S(1)}, u32[]{:S(2)}, u32[]{:S(2)}) collective-permute-start(bf16[80,512]{1,0:T(8,128)(2,1)S(1)} %all_gather.7), channel_id=1, source_target_pairs={{24,0},{28,4},{0,8},{4,12},{8,16},{12,20},{16,24},{20,28},{25,1},{... | collective-permute-start | bytes 245768 | tf_op jit(solution)/shard_map/ppermute | solution.py:12
  131.5 6.5 %collective-permute-start.8 = (bf16[80,512]{1,0:T(8,128)(2,1)S(1)}, bf16[80,512]{1,0:T(8,128)(2,1)S(1)}, u32[]{:S(2)}, u32[]{:S(2)}) collective-permute-start(bf16[80,512]{1,0:T(8,128)(2,1)S(1)} %all_gather.7), channel_id=1, source_target_pairs={{8,0},{12,4},{16,8},{20,12},{24,16},{28,20},{0,24},{4,28},{9,1},{1... | collective-permute-start | bytes 245768 | tf_op jit(solution)/shard_map/ppermute | solution.py:12
  132.2 6.1 %collective-permute-start.7 = (bf16[80,512]{1,0:T(8,128)(2,1)S(1)}, bf16[80,512]{1,0:T(8,128)(2,1)S(1)}, u32[]{:S(2)}, u32[]{:S(2)}) collective-permute-start(bf16[80,512]{1,0:T(8,128)(2,1)S(1)} %all_gather.7), channel_id=1, source_target_pairs={{28,0},{0,4},{4,8},{8,12},{12,16},{16,20},{20,24},{24,28},{29,1},{... | collective-permute-start | bytes 245768 | tf_op jit(solution)/shard_map/ppermute | solution.py:12
  133.0 6.3 %collective-permute-start.6 = (bf16[80,512]{1,0:T(8,128)(2,1)S(1)}, bf16[80,512]{1,0:T(8,128)(2,1)S(1)}, u32[]{:S(2)}, u32[]{:S(2)}) collective-permute-start(bf16[80,512]{1,0:T(8,128)(2,1)S(1)} %all_gather.7), channel_id=1, source_target_pairs={{4,0},{8,4},{12,8},{16,12},{20,16},{24,20},{28,24},{0,28},{5,1},{9... | collective-permute-start | bytes 245768 | tf_op jit(solution)/shard_map/ppermute | solution.py:12
where the time goes:
time: 182 us
  blocking collectives  149 us (82%)
  starting transfers between devices  14.7 us (8%)
  matrix products  7.05 us (4%)
  between operations  4.71 us (3%)
  other arithmetic  2.96 us (2%)
  local copies, waits for them, and re-layouts  2.08 us (1%)
    psum x2, blocking collectives, squares(): return lax.psum(jnp.sum(values * values, axis=1), ('blk', 'grp'))  82.2 us
    psum x1, blocking collectives, on_device(): lax.psum(jnp.sum(direction * image, axis=1), ('blk', 'grp'))  41.3 us
    all_gather x2, blocking collectives, on_device(): own = lax.all_gather(stacked, 'grp', axis=1, tiled=True)  25.9 us
    ppermute x12, starting transfers between devices, passed_along(): return lax.ppermute(block, axis, route)  14.7 us
    dot_general x8, matrix products, kernel_tile(): jnp.dot(row_z.T, col_z, precision=lax.Precision.HIGHEST, preferred_elemen...  5.82 us
  transfers between devices with their start and end apart: 12, of which 1 were waited for; matrix products, arithmetic and copies ran while one was open for 5% of the time, Pallas kernels for 0%

commit v1 on v0

--- a/solution.py
+++ b/solution.py
@@ -73,7 +73,8 @@
     for step in range(ITERS):
         rounded = direction.astype(jnp.bfloat16)
         stacked = jnp.concatenate([points, rounded], axis=0)
-        own = lax.all_gather(stacked, "grp", axis=1, tiled=True)
+        shards = lax.all_gather(stacked, "grp")
+        own = jnp.concatenate(shards, axis=1)
         forward, unused = tile_terms(own_z, own, scales)
         for offset in range(1, maxp + 1):
             for sign in (1, -1):

time: 182 us -> 182 us (level)
  starting transfers between devices: 14.7 us -> 11.2 us
    ppermute x12, starting transfers between devices: 14.7 us -> 11.2 us  [passed_along(): return lax.ppermute(block, axis, route)]
    psum x1, blocking collectives: 41.3 us -> 38.8 us  [on_device(): lax.psum(jnp.sum(direction * image, axis=1), ('blk', 'grp'))]
    all_gather x2, blocking collectives: 25.9 us -> 28.2 us  [on_device(): shards = lax.all_gather(stacked, 'grp')]
    ppermute x12, waiting for transfers between devices: 0.31 us -> 2.13 us  [passed_along(): return lax.ppermute(block, axis, route)]
  transfers between devices with their start and end apart: 12 -> 12, of which waited for: 1 -> 2; matrix products, arithmetic and copies ran while one was open for 5% -> 4% of each run, Pallas kernels for 0% -> 0%
where the time goes in v1:
time: 182 us; the launch traced here: 181 us
  blocking collectives  150 us (82%)
  starting transfers between devices  11.2 us (6%)
  matrix products  7.04 us (4%)
  between operations  4.82 us (3%)
  other arithmetic  2.99 us (2%)
  waiting for transfers between devices  2.13 us (1%)
  local copies, waits for them, and re-layouts  2.09 us (1%)
    psum x2, blocking collectives, squares(): return lax.psum(jnp.sum(values * values, axis=1), ('blk', 'grp'))  83.5 us
    psum x1, blocking collectives, on_device(): lax.psum(jnp.sum(direction * image, axis=1), ('blk', 'grp'))  38.8 us
    all_gather x2, blocking collectives, on_device(): shards = lax.all_gather(stacked, 'grp')  28.2 us
    ppermute x12, starting transfers between devices, passed_along(): return lax.ppermute(block, axis, route)  11.2 us
    dot_general x8, matrix products, kernel_tile(): jnp.dot(row_z.T, col_z, precision=lax.Precision.HIGHEST, preferred_elemen...  5.82 us
  transfers between devices with their start and end apart: 12, of which 2 were waited for; matrix products, arithmetic and copies ran while one was open for 4% of the time, Pallas kernels for 0%

profile of v1, /device:TPU:0, one launch (start us, length us, event | category | flops | bytes accessed | tf_op | source)
XLA Modules:
  0.0 180.9 jit_solution(561359501911999106)
XLA Ops:
  0.6 0.8 convert_element_type.161
  1.4 14.9 %all-gather = bf16[320,128]{1,0:T(8,128)(2,1)S(1)} all-gather(bf16[80,128]{1,0:T(8,128)(2,1)S(1)} %pad_maximum_fusion.1), channel_id=2, replica_groups=mesh['blk'=8,'grp'=4] {'grp'}, dimensions={0}, use_global_device_ids=true | all-gather | bytes 102400 | tf_op jit(solution)/shard_map/all_gather | solution.py:76
  16.4 0.0 copy-start.1
  16.4 0.1 collective-permute-start
  16.5 0.5 collective-permute-start.1
  17.0 2.4 %collective-permute-start.2 = (bf16[80,512]{1,0:T(8,128)(2,1)S(1)}, bf16[80,512]{1,0:T(8,128)(2,1)S(1)}, u32[]{:S(2)}, u32[]{:S(2)}) collective-permute-start(bf16[80,512]{1,0:T(8,128)(2,1)S(1)} %bitcast.224), channel_id=1, source_target_pairs={{8,0},{12,4},{16,8},{20,12},{24,16},{28,20},{0,24},{4,28},{9,1},{1... | collective-permute-start | bytes 245768 | tf_op jit(solution)/shard_map/ppermute | solution.py:12
  19.4 0.0 collective-permute-start.3
  19.4 1.3 collective-permute-start.4
  20.7 0.1 multiply_reduce_fusion.28
  20.8 0.1 fusion.98
  21.0 0.6 multiply_convert_fusion.13
  21.6 0.0 copy-start.4
  21.6 0.2 fusion.93
  21.8 0.0 collective-permute-done
  21.8 0.9 collective-permute-start.5
  22.7 0.6 constant_dynamic-slice_fusion.5
  24.6 0.7 constant_dynamic-slice_fusion.1
  27.9 0.0 collective-permute-done.1
  27.9 1.1 conditional.13
  27.9 0.1 multiply_reduce_fusion.2
  28.0 0.8 multiply_convert_fusion.1
  28.8 0.2 convolution_bitcast_fusion.1
  29.1 1.1 conditional.16
  29.1 0.1 multiply_reduce_fusion.8
  29.2 0.8 multiply_convert_fusion.4
  30.0 0.2 convolution_bitcast_fusion.4
  30.1 0.0 copy-start
  30.1 1.1 conditional.17
  30.2 0.1 multiply_reduce_fusion.10
  30.3 0.8 multiply_convert_fusion.5
  31.0 0.2 convolution_bitcast_fusion.5
  31.2 0.6 copy-done.3
  31.9 0.1 multiply_reduce_fusion.26
  32.0 42.0 %all-reduce = (f32[64]{0:T(128)S(1)}, f32[64]{0:T(128)S(1)}) all-reduce(f32[64]{0:T(128)S(1)} %get-tuple-element.357, f32[64]{0:T(128)S(1)} %get-tuple-element.356), channel_id=1, replica_groups=mesh['blk'=8,'grp'=4] {'blk','grp'}, use_global_device_ids=true, to_apply=%region_1.0 | all-reduce | flops 128 | bytes 1024 | tf_op jit(solution)/shard_map/psum | solution.py:67
  74.0 0.2 multiply_reduce_fusion.25
  74.2 41.4 %psum.30 = f32[64]{0:T(128)S(1)} all-reduce(f32[64]{0:T(128)S(1)} %multiply_reduce_fusion.25), channel_id=1, replica_groups=mesh['blk'=8,'grp'=4] {'blk','grp'}, use_global_device_ids=true, to_apply=%region_31.32 | all-reduce | flops 64 | bytes 512 | tf_op jit(solution)/shard_map/psum | solution.py:67
  115.6 0.1 fusion.102
  115.7 13.2 %all-gather.1 = bf16[320,128]{1,0:T(8,128)(2,1)S(1)} all-gather(bf16[80,128]{1,0:T(8,128)(2,1)S(1)} %pad_maximum_fusion), channel_id=3, replica_groups=mesh['blk'=8,'grp'=4] {'grp'}, dimensions={0}, use_global_device_ids=true | all-gather | bytes 102400 | tf_op jit(solution)/shard_map/all_gather | solution.py:76
  129.0 0.1 fusion.99
  129.1 0.1 collective-permute-start.6
  129.2 0.5 collective-permute-start.7
  129.7 1.8 %collective-permute-start.8 = (bf16[80,512]{1,0:T(8,128)(2,1)S(1)}, bf16[80,512]{1,0:T(8,128)(2,1)S(1)}, u32[]{:S(2)}, u32[]{:S(2)}) collective-permute-start(bf16[80,512]{1,0:T(8,128)(2,1)S(1)} %bitcast.230), channel_id=1, source_target_pairs={{8,0},{12,4},{16,8},{20,12},{24,16},{28,20},{0,24},{4,28},{9,1},{1... | collective-permute-start | bytes 245768 | tf_op jit(solution)/shard_map/ppermute | solution.py:12
  131.5 0.4 collective-permute-start.9
  132.0 1.9 %collective-permute-start.10 = (bf16[80,512]{1,0:T(8,128)(2,1)S(1)}, bf16[80,512]{1,0:T(8,128)(2,1)S(1)}, u32[]{:S(2)}, u32[]{:S(2)}) collective-permute-start(bf16[80,512]{1,0:T(8,128)(2,1)S(1)} %bitcast.232), channel_id=1, source_target_pairs={{12,0},{16,4},{20,8},{24,12},{28,16},{0,20},{4,24},{8,28},{13,1},{... | collective-permute-start | bytes 245768 | tf_op jit(solution)/shard_map/ppermute | solution.py:12
  133.8 0.6 multiply_convert_fusion.12
  134.5 1.2 collective-permute-start.11
  135.8 0.2 fusion.90
  136.0 1.1 conditional.19
  136.0 0.1 multiply_reduce_fusion.14
  136.1 0.8 multiply_convert_fusion.7
  136.9 0.2 convolution_bitcast_fusion.7
  137.1 1.3 collective-permute-done.9
  138.4 0.8 collective-permute-done.10
  139.2 1.0 conditional.22
  139.2 0.1 multiply_reduce_fusion.20
  139.3 0.8 multiply_convert_fusion.10
  140.1 0.2 convolution_bitcast_fusion.10
  140.2 1.1 conditional.23
  140.2 0.1 multiply_reduce_fusion.22
  140.4 0.8 multiply_convert_fusion.11
  141.1 0.2 convolution_bitcast_fusion.11
  141.3 0.1 multiply_reduce_fusion.24
  141.4 38.8 %psum.31 = f32[64]{0:T(128)S(1)} all-reduce(f32[64]{0:T(128)S(1)} %get-tuple-element.360), channel_id=1, replica_groups=mesh['blk'=8,'grp'=4] {'blk','grp'}, use_global_device_ids=true, to_apply=%region_58.59 | all-reduce | flops 64 | bytes 512 | tf_op jit(solution)/shard_map/psum | solution.py:96
  180.2 0.7 multiply_subtract_fusion
  (46 shorter events, 0.5 us)
Async XLA Ops:
  0.6 0.8 copy-start.2
  16.4 4.3 %copy-start.1 = (f32[16]{0:T(128)S(1)}, f32[16]{0:T(128)}, u32[]{:S(2)}) copy-start(f32[16]{0:T(128)} %param.32) | copy-start | bytes 196
  16.4 5.4 %collective-permute-start = (bf16[80,512]{1,0:T(8,128)(2,1)S(1)}, bf16[80,512]{1,0:T(8,128)(2,1)S(1)}, u32[]{:S(2)}, u32[]{:S(2)}) collective-permute-start(bf16[80,512]{1,0:T(8,128)(2,1)S(1)} %bitcast.222), channel_id=1, source_target_pairs={{4,0},{8,4},{12,8},{16,12},{20,16},{24,20},{28,24},{0,28},{5,1},{9... | collective-permute-start | bytes 245768 | tf_op jit(solution)/shard_map/ppermute | solution.py:12
  16.5 11.4 %collective-permute-start.1 = (bf16[80,512]{1,0:T(8,128)(2,1)S(1)}, bf16[80,512]{1,0:T(8,128)(2,1)S(1)}, u32[]{:S(2)}, u32[]{:S(2)}) collective-permute-start(bf16[80,512]{1,0:T(8,128)(2,1)S(1)} %bitcast.223), channel_id=1, source_target_pairs={{28,0},{0,4},{4,8},{8,12},{12,16},{16,20},{20,24},{24,28},{29,1},{... | collective-permute-start | bytes 245768 | tf_op jit(solution)/shard_map/ppermute | solution.py:12
  17.0 12.0 %collective-permute-start.2 = (bf16[80,512]{1,0:T(8,128)(2,1)S(1)}, bf16[80,512]{1,0:T(8,128)(2,1)S(1)}, u32[]{:S(2)}, u32[]{:S(2)}) collective-permute-start(bf16[80,512]{1,0:T(8,128)(2,1)S(1)} %bitcast.224), channel_id=1, source_target_pairs={{8,0},{12,4},{16,8},{20,12},{24,16},{28,20},{0,24},{4,28},{9,1},{1... | collective-permute-start | bytes 245768 | tf_op jit(solution)/shard_map/ppermute | solution.py:12
  19.4 9.6 %collective-permute-start.3 = (bf16[80,512]{1,0:T(8,128)(2,1)S(1)}, bf16[80,512]{1,0:T(8,128)(2,1)S(1)}, u32[]{:S(2)}, u32[]{:S(2)}) collective-permute-start(bf16[80,512]{1,0:T(8,128)(2,1)S(1)} %bitcast.225), channel_id=1, source_target_pairs={{24,0},{28,4},{0,8},{4,12},{8,16},{12,20},{16,24},{20,28},{25,1},{... | collective-permute-start | bytes 245768 | tf_op jit(solution)/shard_map/ppermute | solution.py:12
  19.4 9.6 %collective-permute-start.4 = (bf16[80,512]{1,0:T(8,128)(2,1)S(1)}, bf16[80,512]{1,0:T(8,128)(2,1)S(1)}, u32[]{:S(2)}, u32[]{:S(2)}) collective-permute-start(bf16[80,512]{1,0:T(8,128)(2,1)S(1)} %bitcast.226), channel_id=1, source_target_pairs={{12,0},{16,4},{20,8},{24,12},{28,16},{0,20},{4,24},{8,28},{13,1},{... | collective-permute-start | bytes 245768 | tf_op jit(solution)/shard_map/ppermute | solution.py:12
  21.6 1.1 copy-start.4
  21.8 8.3 %collective-permute-start.5 = (bf16[80,512]{1,0:T(8,128)(2,1)S(1)}, bf16[80,512]{1,0:T(8,128)(2,1)S(1)}, u32[]{:S(2)}, u32[]{:S(2)}) collective-permute-start(bf16[80,512]{1,0:T(8,128)(2,1)S(1)} %bitcast.227), channel_id=1, source_target_pairs={{20,0},{24,4},{28,8},{0,12},{4,16},{8,20},{12,24},{16,28},{21,1},{... | collective-permute-start | bytes 245768 | tf_op jit(solution)/shard_map/ppermute | solution.py:12
  30.1 1.1 copy-start
  31.2 0.7 copy-start.3
  129.1 5.4 %collective-permute-start.6 = (bf16[80,512]{1,0:T(8,128)(2,1)S(1)}, bf16[80,512]{1,0:T(8,128)(2,1)S(1)}, u32[]{:S(2)}, u32[]{:S(2)}) collective-permute-start(bf16[80,512]{1,0:T(8,128)(2,1)S(1)} %bitcast.228), channel_id=1, source_target_pairs={{4,0},{8,4},{12,8},{16,12},{20,16},{24,20},{28,24},{0,28},{5,1},{9... | collective-permute-start | bytes 245768 | tf_op jit(solution)/shard_map/ppermute | solution.py:12
  129.2 6.8 %collective-permute-start.7 = (bf16[80,512]{1,0:T(8,128)(2,1)S(1)}, bf16[80,512]{1,0:T(8,128)(2,1)S(1)}, u32[]{:S(2)}, u32[]{:S(2)}) collective-permute-start(bf16[80,512]{1,0:T(8,128)(2,1)S(1)} %bitcast.229), channel_id=1, source_target_pairs={{28,0},{0,4},{4,8},{8,12},{12,16},{16,20},{20,24},{24,28},{29,1},{... | collective-permute-start | bytes 245768 | tf_op jit(solution)/shard_map/ppermute | solution.py:12
  129.7 7.3 %collective-permute-start.8 = (bf16[80,512]{1,0:T(8,128)(2,1)S(1)}, bf16[80,512]{1,0:T(8,128)(2,1)S(1)}, u32[]{:S(2)}, u32[]{:S(2)}) collective-permute-start(bf16[80,512]{1,0:T(8,128)(2,1)S(1)} %bitcast.230), channel_id=1, source_target_pairs={{8,0},{12,4},{16,8},{20,12},{24,16},{28,20},{0,24},{4,28},{9,1},{1... | collective-permute-start | bytes 245768 | tf_op jit(solution)/shard_map/ppermute | solution.py:12
  131.5 6.9 %collective-permute-start.9 = (bf16[80,512]{1,0:T(8,128)(2,1)S(1)}, bf16[80,512]{1,0:T(8,128)(2,1)S(1)}, u32[]{:S(2)}, u32[]{:S(2)}) collective-permute-start(bf16[80,512]{1,0:T(8,128)(2,1)S(1)} %bitcast.231), channel_id=1, source_target_pairs={{24,0},{28,4},{0,8},{4,12},{8,16},{12,20},{16,24},{20,28},{25,1},{... | collective-permute-start | bytes 245768 | tf_op jit(solution)/shard_map/ppermute | solution.py:12
  132.0 7.2 %collective-permute-start.10 = (bf16[80,512]{1,0:T(8,128)(2,1)S(1)}, bf16[80,512]{1,0:T(8,128)(2,1)S(1)}, u32[]{:S(2)}, u32[]{:S(2)}) collective-permute-start(bf16[80,512]{1,0:T(8,128)(2,1)S(1)} %bitcast.232), channel_id=1, source_target_pairs={{12,0},{16,4},{20,8},{24,12},{28,16},{0,20},{4,24},{8,28},{13,1},{... | collective-permute-start | bytes 245768 | tf_op jit(solution)/shard_map/ppermute | solution.py:12
  134.5 5.7 %collective-permute-start.11 = (bf16[80,512]{1,0:T(8,128)(2,1)S(1)}, bf16[80,512]{1,0:T(8,128)(2,1)S(1)}, u32[]{:S(2)}, u32[]{:S(2)}) collective-permute-start(bf16[80,512]{1,0:T(8,128)(2,1)S(1)} %bitcast.233), channel_id=1, source_target_pairs={{20,0},{24,4},{28,8},{0,12},{4,16},{8,20},{12,24},{16,28},{21,1},{... | collective-permute-start | bytes 245768 | tf_op jit(solution)/shard_map/ppermute | solution.py:12
